TPU v7x, 256 devices: a whole 4x4x8 slice. The times are simulated.
256 devices in a mesh: rep: 4 (over z_lo), fsdp: 64 (over x, z_hi, y, core).
Axes of the slice: x: 4, y: 4, z: 8 (z_hi: 2, z_lo: 4; z = z_hi * 4 + z_lo), core: 2. Of those that a mesh axis runs over, the one named last changes fastest.
Arguments:
- latents: bfloat16 [256, 16, 16, 640], P(('rep', 'fsdp')), may hold values from -6 to 6
- cotangent: bfloat16 [256, 16, 16, 640], P(('rep', 'fsdp')), may hold values from -6 to 6
- conv_weight: bfloat16 [4, 5760, 640], P('rep', 'fsdp'), may hold values from -0.078125 to 0.078125
- norm_gain: float32 [4, 640], P('rep'), may hold values from 0.5 to 1.5
- norm_shift: float32 [4, 640], P('rep'), may hold values from -3 to 3
- partner_bit: int32 [64], replicated, may hold values from 0 to 1
Outputs:
- block_out: bfloat16 [256, 16, 16, 640], P(('rep', 'fsdp'))
- input_grad: bfloat16 [256, 16, 16, 640], P(('rep', 'fsdp'))
- weight_grad: float32 [4, 5760, 640], P('rep', 'fsdp')
- norm_grad: float32 [4, 2, 640], P('rep')
Inputs may be any that keep to these rules, and one draw needn't show every extreme that they name: In row shard f, replica r is paired with replica r with bit partner_bit[f] of its index flipped.
All inputs are finite; a program needn't handle non-finite values.
Results may differ from a plain program's by a relative error of at most 0.0065.
Values may be sent and summed in bfloat16 or wider, within the bound.
A program may use at most 128 MiB of HBM per device.

v0:
```python
import jax
import jax.numpy as jnp
from jax import lax
from jax.sharding import PartitionSpec as P

GROUPS = 32


def partner(value, axis, stride):
    mask = 2**stride
    pairs = [(source, source ^ mask) for source in range(lax.axis_size(axis))]
    return lax.ppermute(value, axis, pairs)


def norm_forward(values_in, gain, shift, groups):
    count, side, chans = (values_in.shape[0], values_in.shape[1], values_in.shape[3])
    values = values_in.astype(jnp.float32).reshape(count, side * side, groups, chans // groups)
    center = jnp.mean(values, axis=(1, 3), keepdims=True)
    spread = jnp.mean(jnp.square(values - center), axis=(1, 3), keepdims=True)
    scale_inv = lax.rsqrt(spread + 1e-05)
    normed = (values - center) * scale_inv
    pre_act = normed * gain.reshape(groups, -1) + shift.reshape(groups, -1)
    return (normed, scale_inv, pre_act)


def make_patches(activation):
    count, side, chans = (activation.shape[0], activation.shape[1], activation.shape[3])
    padded = jnp.pad(activation, ((0, 0), (1, 1), (1, 1), (0, 0)))
    pieces = [
        padded[:, row_off : row_off + side, col_off : col_off + side, :]
        for row_off in range(3)
        for col_off in range(3)
    ]
    return jnp.concatenate(pieces, axis=-1).reshape(count * side * side, 9 * chans)


def fold_patches(patch_grad, count, side, chans):
    grads = patch_grad.reshape(count, side, side, 9, chans)
    total = jnp.zeros((count, side + 2, side + 2, chans), jnp.float32)
    for row_off in range(3):
        for col_off in range(3):
            tap = grads[:, :, :, row_off * 3 + col_off, :]
            total = total + jnp.pad(
                tap, ((0, 0), (row_off, 2 - row_off), (col_off, 2 - col_off), (0, 0))
            )
    return total[:, 1:-1, 1:-1, :]


def backward_rest(act_grad, normed, scale_inv, pre_act, gain, groups, inv_batch):
    count, side, chans = (act_grad.shape[0], act_grad.shape[1], act_grad.shape[3])
    act_grad = act_grad.reshape(count, side * side, groups, chans // groups)
    sigma = jax.nn.sigmoid(pre_act)
    pre_grad = act_grad * sigma * (1.0 + pre_act * (1.0 - sigma))
    gain_grad = jnp.sum(pre_grad * normed, axis=(0, 1)).reshape(-1) * inv_batch
    shift_grad = jnp.sum(pre_grad, axis=(0, 1)).reshape(-1) * inv_batch
    normed_grad = pre_grad * gain.reshape(groups, -1)
    first = jnp.mean(normed_grad, axis=(1, 3), keepdims=True)
    second = jnp.mean(normed_grad * normed, axis=(1, 3), keepdims=True)
    input_grad = scale_inv * (normed_grad - first - normed * second)
    return (
        input_grad.reshape(count, side, side, chans).astype(jnp.bfloat16),
        jnp.stack([gain_grad, shift_grad]),
    )


def shards(latents, cotangent, conv_weight, norm_gain, norm_shift, partner_bit):
    count, side, chans = (latents.shape[0], latents.shape[1], latents.shape[3])
    shard_total = lax.axis_size("fsdp")
    inv_batch = 1.0 / (count * shard_total)
    gain = norm_gain[0]
    normed, scale_inv, pre_act = norm_forward(latents, gain, norm_shift[0], GROUPS)
    activation = jax.nn.silu(pre_act).astype(jnp.bfloat16).reshape(count, side, side, chans)
    patches = make_patches(activation)
    cot_rows = cotangent.reshape(count * side * side, chans)
    weight_rows = conv_weight[0]
    output = jnp.dot(
        patches,
        lax.all_gather(weight_rows, "fsdp", axis=0, tiled=True),
        preferred_element_type=jnp.float32,
    )
    patch_grad = lax.dot_general(
        cot_rows,
        lax.all_gather(weight_rows, "fsdp", axis=0, tiled=True),
        (((1,), (1,)), ((), ())),
        preferred_element_type=jnp.float32,
    )
    block_out = output.astype(jnp.bfloat16).reshape(count, side, side, chans)
    act_grad = fold_patches(patch_grad, count, side, chans)
    input_grad, norm_term = backward_rest(
        act_grad, normed, scale_inv, pre_act, gain, GROUPS, inv_batch
    )
    weight_term = (
        lax.dot_general(
            patches, cot_rows, (((0,), (0,)), ((), ())), preferred_element_type=jnp.float32
        )
        * inv_batch
    )
    shard_rows = weight_rows.shape[0]
    term_pieces = weight_term.reshape(shard_total, shard_rows, chans)
    received = lax.all_to_all(
        term_pieces.astype(jnp.bfloat16), "fsdp", split_axis=0, concat_axis=0, tiled=True
    ).astype(term_pieces.dtype)
    weight_shard = jnp.sum(received, axis=0)
    bit_count = lax.axis_size("rep").bit_length() - 1
    shard_bit = lax.dynamic_index_in_dim(partner_bit, lax.axis_index("fsdp"), 0, keepdims=False)
    norm_bit = partner_bit[0]
    norm_total = lax.psum(norm_term, "fsdp")
    weight_avg, norm_avg = (weight_shard, norm_total)
    for bit_index in range(bit_count):
        other_weight, other_norm = (
            partner(weight_shard.astype(jnp.bfloat16), "rep", bit_index).astype(weight_shard.dtype),
            partner(norm_total.astype(jnp.bfloat16), "rep", bit_index).astype(norm_total.dtype),
        )
        weight_avg = jnp.where(
            shard_bit == bit_index, 0.5 * (weight_shard + other_weight), weight_avg
        )
        norm_avg = jnp.where(norm_bit == bit_index, 0.5 * (norm_total + other_norm), norm_avg)
    return (block_out, input_grad, weight_avg[None], norm_avg[None])


def solution(mesh):
    in_specs = (
        P(("rep", "fsdp"), None, None, None),
        P(("rep", "fsdp"), None, None, None),
        P("rep", "fsdp", None),
        P("rep", None),
        P("rep", None),
        P(),
    )
    out_specs = (
        P(("rep", "fsdp"), None, None, None),
        P(("rep", "fsdp"), None, None, None),
        P("rep", "fsdp", None),
        P("rep", None, None),
    )
    return jax.shard_map(shards, mesh=mesh, in_specs=in_specs, out_specs=out_specs, check_vma=False)
```

profile of v0, /device:TPU:0, one launch (start us, length us, event | category | flops | bytes accessed | tf_op | source)
XLA Modules:
  0.0 605.6 jit_solution(758910239517122541)
XLA Ops:
  7.2 1.8 copy.35
  9.1 1.0 convert_reduce_fusion.1
  10.5 1.1 fusion.28
  13.4 144.8 %all-gather.3.cloned.1.call-done = bf16[1,5760,640]{2,0,1:T(2,128)(2,1)} async-done(((bf16[1,90,640]{2,0,1:T(2,128)(2,1)}), bf16[1,5760,640]{2,0,1:T(2,128)(2,1)}) %all-gather.3.cloned.1.call-update) | async-done | bytes 7372816 | tf_op jit(solution)/shard_map/all_gather | solution.py:78
  158.2 9.4 %copy.45 = bf16[1,5760,640]{2,1,0:T(8,128)(2,1)} copy(bf16[1,5760,640]{2,0,1:T(2,128)(2,1)} %all-gather.3.cloned.1.call-done) | data formatting | bytes 14745600
  167.6 5.6 convolution_bitcast_fusion
  173.9 0.8 copy-done.2
  174.6 0.9 fusion.27
  176.2 1.1 constant_dynamic-update-slice_fusion.9
  177.3 5.5 fusion
  182.8 9.1 %convert_element_type.71 = bf16[64,90,640]{2,1,0:T(8,128)(2,1)} reshape(bf16[5760,640]{1,0:T(8,128)(2,1)} %fusion) | data formatting | bytes 14745600 | tf_op jit(solution)/shard_map/convert_element_type | solution.py:101
  191.9 6.5 %all-to-all-start = ((bf16[64,90,640]{2,1,0:T(8,128)(2,1)}), bf16[64,90,640]{2,1,0:T(8,128)(2,1)}, u32[]{:S(2)}, u32[]{:S(2)}) async-start(bf16[64,90,640]{2,1,0:T(8,128)(2,1)} %convert_element_type.71), calls=%async_computation | async-start | bytes 15728640 | tf_op jit(solution)/shard_map/all_to_all | solution.py:100
  201.7 354.6 %psum.7 = f32[2,640]{1,0:T(2,128)S(1)} all-reduce(f32[2,640]{1,0:T(2,128)S(1)} %pad_maximum_fusion), channel_id=1, replica_groups=mesh['rep'=4,'fsdp'=64] {'fsdp'}, use_global_device_ids=true, to_apply=%region_11.12 | all-reduce | flops 1280 | bytes 10240 | tf_op jit(solution)/shard_map/psum | solution.py:107
  556.3 9.9 %collective-permute-start.3 = (bf16[2,640]{1,0:T(2,128)(2,1)S(1)}, bf16[2,640]{1,0:T(2,128)(2,1)S(1)}, u32[]{:S(2)}, u32[]{:S(2)}) collective-permute-start(bf16[2,640]{1,0:T(2,128)(2,1)S(1)} %convert_element_type.76), channel_id=1, source_target_pairs={{0,64},{64,0},{128,192},{192,128},{1,65},{65,1},{129,193},{193,129... | collective-permute-start | bytes 7688 | tf_op jit(solution)/shard_map/ppermute | solution.py:12
  566.2 8.0 %collective-permute-start.2 = (bf16[2,640]{1,0:T(2,128)(2,1)S(1)}, bf16[2,640]{1,0:T(2,128)(2,1)S(1)}, u32[]{:S(2)}, u32[]{:S(2)}) collective-permute-start(bf16[2,640]{1,0:T(2,128)(2,1)S(1)} %convert_element_type.76), channel_id=1, source_target_pairs={{0,128},{64,192},{128,0},{192,64},{1,129},{65,193},{129,1},{193,65... | collective-permute-start | bytes 7688 | tf_op jit(solution)/shard_map/ppermute | solution.py:12
  575.0 1.0 constant_dynamic-update-slice_fusion.8
  576.0 1.0 constant_dynamic-update-slice_fusion.7
  577.4 0.9 fusion.26
  578.3 6.4 %fusion.4 = bf16[256,640]{1,0:T(8,128)(2,1)} fusion(bf16[256,5760]{1,0:T(8,128)(2,1)S(1)} %constant_dynamic-update-slice_fusion, bf16[1,5760,640]{2,1,0:T(8,128)(2,1)} %copy.45), kind=kOutput, calls=%fused_computation.7 | convolution fusion | flops 1887600640 | bytes 10649600 | tf_op jit(solution)/shard_map/dot_general | solution.py:76
  584.7 4.5 convert_reduce_fusion
  589.2 1.8 collective-permute-start.1
  591.6 2.5 collective-permute-done.1
  594.2 3.7 collective-permute-done
  597.9 0.8 broadcast_in_dim.4
  (63 shorter events, 5.9 us)
Async XLA Ops:
  7.2 160.5 %copy-start = (bf16[1,16,16,640]{3,2,1,0:T(8,128)(2,1)S(1)}, bf16[1,16,16,640]{3,2,1,0:T(8,128)(2,1)}, u32[]{:S(2)}) copy-start(bf16[1,16,16,640]{3,2,1,0:T(8,128)(2,1)} %param.7) | copy-start | bytes 983044
  7.2 151.0 %all-gather.3.cloned.1.call-start = ((), (), s32[]{:S(2)}) async-start(), calls=%async_computation.1 | async-start | bytes 14976000 | tf_op jit(solution)/shard_map/all_gather | solution.py:78
  173.7 1.0 copy-start.2
  191.9 6.5 %copy-start.4 = (s32[64]{0:T(128)S(1)}, s32[64]{0:T(128)}, u32[]{:S(2)}) copy-start(s32[64]{0:T(128)} %param.11) | copy-start | bytes 772
  191.9 385.1 %copy-start.3 = (bf16[1,16,16,640]{3,2,1,0:T(8,128)(2,1)S(1)}, bf16[1,16,16,640]{3,2,1,0:T(8,128)(2,1)}, u32[]{:S(2)}) copy-start(bf16[1,16,16,640]{3,2,1,0:T(8,128)(2,1)} %get-tuple-element.21) | copy-start | bytes 983044
  191.9 392.8 %all-to-all-start = ((bf16[64,90,640]{2,1,0:T(8,128)(2,1)}), bf16[64,90,640]{2,1,0:T(8,128)(2,1)}, u32[]{:S(2)}, u32[]{:S(2)}) async-start(bf16[64,90,640]{2,1,0:T(8,128)(2,1)} %convert_element_type.71), calls=%async_computation | async-start | bytes 15728640 | tf_op jit(solution)/shard_map/all_to_all | solution.py:100
  556.3 34.7 %collective-permute-start.3 = (bf16[2,640]{1,0:T(2,128)(2,1)S(1)}, bf16[2,640]{1,0:T(2,128)(2,1)S(1)}, u32[]{:S(2)}, u32[]{:S(2)}) collective-permute-start(bf16[2,640]{1,0:T(2,128)(2,1)S(1)} %convert_element_type.76), channel_id=1, source_target_pairs={{0,64},{64,0},{128,192},{192,128},{1,65},{65,1},{129,193},{193,129... | collective-permute-start | bytes 7688 | tf_op jit(solution)/shard_map/ppermute | solution.py:12
  566.2 24.9 %collective-permute-start.2 = (bf16[2,640]{1,0:T(2,128)(2,1)S(1)}, bf16[2,640]{1,0:T(2,128)(2,1)S(1)}, u32[]{:S(2)}, u32[]{:S(2)}) collective-permute-start(bf16[2,640]{1,0:T(2,128)(2,1)S(1)} %convert_element_type.76), channel_id=1, source_target_pairs={{0,128},{64,192},{128,0},{192,64},{1,129},{65,193},{129,1},{193,65... | collective-permute-start | bytes 7688 | tf_op jit(solution)/shard_map/ppermute | solution.py:12
  578.3 20.5 %copy-start.1 = (bf16[1,16,16,640]{3,2,1,0:T(8,128)(2,1)S(1)}, bf16[1,16,16,640]{3,2,1,0:T(8,128)(2,1)}, u32[]{:S(2)}) copy-start(bf16[1,16,16,640]{3,2,1,0:T(8,128)(2,1)} %param.7) | copy-start | bytes 983044
  589.2 5.0 collective-permute-start.1
  591.0 6.8 %collective-permute-start = (bf16[90,640]{1,0:T(8,128)(2,1)S(1)}, bf16[90,640]{1,0:T(8,128)(2,1)S(1)}, u32[]{:S(2)}, u32[]{:S(2)}) collective-permute-start(bf16[90,640]{1,0:T(8,128)(2,1)S(1)} %convert_element_type.73), channel_id=1, source_target_pairs={{0,128},{64,192},{128,0},{192,64},{1,129},{65,193},{129,1},{193,65... | collective-permute-start | bytes 345608 | tf_op jit(solution)/shard_map/ppermute | solution.py:12
Sparse Core Ops, SparseCore 0:
  12.1 146.0 all-gather.2
where the time goes:
time: 606 us
  blocking collectives  355 us (59%)
  waiting for transfers between devices  151 us (25%)
  local copies, waits for them, and re-layouts  28.1 us (5%)
  starting transfers between devices  26.3 us (4%)
  matrix products  17.5 us (3%)
  between operations  16.9 us (3%)
  other arithmetic  11.2 us (2%)
    psum x1, blocking collectives, shards(): norm_total = lax.psum(norm_term, 'fsdp')  355 us
    all_gather x1, waiting for transfers between devices, shards(): lax.all_gather(weight_rows, 'fsdp', axis=0, tiled=True)  145 us
    ppermute x4, starting transfers between devices, partner(): return lax.ppermute(value, axis, pairs)  19.7 us
    unnamed x28, local copies, waits for them, and re-layouts  14.9 us
  transfers between devices with their start and end apart: 6, of which 3 were waited for; matrix products, arithmetic and copies ran while one was open for 3% of the time, Pallas kernels for 0%

commit v1 on v0

--- a/solution.py
+++ b/solution.py
@@ -75,7 +75,9 @@
     weight_rows = conv_weight[0]
     output = jnp.dot(
         patches,
-        lax.all_gather(weight_rows, "fsdp", axis=0, tiled=True),
+        jnp.concatenate(
+            lax.all_to_all(jnp.stack([weight_rows] * lax.axis_size("fsdp")), "fsdp", 0, 0), axis=0
+        ),
         preferred_element_type=jnp.float32,
     )
     patch_grad = lax.dot_general(

time: 606 us -> 745 us (1.23)
  waiting for transfers between devices: 151 us -> 261 us
  blocking collectives: 355 us -> 370 us
  local copies, waits for them, and re-layouts: 28.1 us -> 41.3 us
    all_gather x1, waiting for transfers between devices: 145 us -> 258 us  [shards(): lax.all_gather(weight_rows, 'fsdp', axis=0, tiled=True)]
    psum x1, blocking collectives: 355 us -> 370 us  [shards(): norm_total = lax.psum(norm_term, 'fsdp')]
    ppermute x4, starting transfers between devices: 19.7 us -> 5.12 us  [partner(): return lax.ppermute(value, axis, pairs)]
    all_to_all x0 -> x1, starting transfers between devices: none -> 13.2 us  [shards(): lax.all_to_all(jnp.stack([weight_rows] * lax.axis_size('fsdp')), 'fsdp',...]
    reshape x0 -> x1, local copies, waits for them, and re-layouts: none -> 9.22 us  [shards(): jnp.concatenate(lax.all_to_all(jnp.stack([weight_rows] * lax.axis_size('f...]
  transfers between devices with their start and end apart: 6 -> 7, of which waited for: 3 -> 3; matrix products, arithmetic and copies ran while one was open for 3% -> 9% of each run, Pallas kernels for 0% -> 0%
where the time goes in v1:
time: 745 us; the launch traced here: 743 us
  blocking collectives  370 us (50%)
  waiting for transfers between devices  261 us (35%)
  local copies, waits for them, and re-layouts  41.3 us (6%)
  starting transfers between devices  28.4 us (4%)
  matrix products  17.5 us (2%)
  between operations  17 us (2%)
  other arithmetic  7.86 us (1%)
    psum x1, blocking collectives, shards(): norm_total = lax.psum(norm_term, 'fsdp')  370 us
    all_gather x1, waiting for transfers between devices, shards(): lax.all_gather(weight_rows, 'fsdp', axis=0, tiled=True)  258 us
  transfers between devices with their start and end apart: 7, of which 3 were waited for; matrix products, arithmetic and copies ran while one was open for 9% of the time, Pallas kernels for 0%

profile of v1, /device:TPU:0, one launch (start us, length us, event | category | flops | bytes accessed | tf_op | source)
XLA Modules:
  0.0 743.2 jit_solution(6781821197551256848)
XLA Ops:
  7.2 1.8 copy.35
  9.1 4.7 stack.8
  13.7 13.2 %all-to-all-start = ((bf16[64,90,640]{2,1,0:T(8,128)(2,1)}), bf16[64,90,640]{2,1,0:T(8,128)(2,1)}, u32[]{:S(2)}, u32[]{:S(2)}) async-start(bf16[64,90,640]{2,1,0:T(8,128)(2,1)} %stack.8), calls=%async_computation | async-start | bytes 15728640 | tf_op jit(solution)/shard_map/all_to_all | solution.py:79
  28.0 258.1 %all-gather.3.cloned.1.call-done = bf16[1,5760,640]{2,0,1:T(2,128)(2,1)} async-done(((bf16[1,90,640]{2,0,1:T(2,128)(2,1)}), bf16[1,5760,640]{2,0,1:T(2,128)(2,1)}) %all-gather.3.cloned.1.call-update) | async-done | bytes 7372816 | tf_op jit(solution)/shard_map/all_gather | solution.py:85
  286.1 9.5 %copy.45 = bf16[1,5760,640]{2,1,0:T(8,128)(2,1)} copy(bf16[1,5760,640]{2,0,1:T(2,128)(2,1)} %all-gather.3.cloned.1.call-done) | data formatting | bytes 14745600
  295.6 5.6 convolution_bitcast_fusion
  301.8 0.9 fusion.22
  303.3 1.1 constant_dynamic-update-slice_fusion.9
  304.4 5.6 fusion
  310.0 9.1 %convert_element_type.71 = bf16[64,90,640]{2,1,0:T(8,128)(2,1)} reshape(bf16[5760,640]{1,0:T(8,128)(2,1)} %fusion) | data formatting | bytes 14745600 | tf_op jit(solution)/shard_map/convert_element_type | solution.py:103
  319.1 10.0 %all-to-all-start.1 = ((bf16[64,90,640]{2,1,0:T(8,128)(2,1)}), bf16[64,90,640]{2,1,0:T(8,128)(2,1)}, u32[]{:S(2)}, u32[]{:S(2)}) async-start(bf16[64,90,640]{2,1,0:T(8,128)(2,1)} %convert_element_type.71), calls=%async_computation.1 | async-start | bytes 15728640 | tf_op jit(solution)/shard_map/all_to_all | solution.py:102
  332.4 369.9 %psum.7 = f32[2,640]{1,0:T(2,128)S(1)} all-reduce(f32[2,640]{1,0:T(2,128)S(1)} %pad_maximum_fusion), channel_id=1, replica_groups=mesh['rep'=4,'fsdp'=64] {'fsdp'}, use_global_device_ids=true, to_apply=%region_11.12 | all-reduce | flops 1280 | bytes 10240 | tf_op jit(solution)/shard_map/psum | solution.py:109
  702.4 1.2 collective-permute-start.3
  704.4 9.2 %reshape.219 = bf16[5760,640]{1,0:T(8,128)(2,1)} reshape(bf16[64,90,640]{2,1,0:T(8,128)(2,1)} %all-to-all-done) | data formatting | bytes 14745600 | tf_op jit(solution)/shard_map/reshape | solution.py:78
  713.6 1.0 constant_dynamic-update-slice_fusion.8
  714.7 1.0 constant_dynamic-update-slice_fusion.7
  716.0 0.9 fusion.21
  716.9 6.4 convolution_convert_fusion
  723.3 4.5 convert_reduce_fusion
  727.8 1.8 collective-permute-start
  729.6 2.0 collective-permute-start.1
  731.7 0.6 select_bitcast_fusion
  732.3 2.8 collective-permute-done
  735.5 0.8 broadcast_in_dim.4
  (71 shorter events, 4.4 us)
Async XLA Ops:
  7.2 288.4 %copy-start = (bf16[1,16,16,640]{3,2,1,0:T(8,128)(2,1)S(1)}, bf16[1,16,16,640]{3,2,1,0:T(8,128)(2,1)}, u32[]{:S(2)}) copy-start(bf16[1,16,16,640]{3,2,1,0:T(8,128)(2,1)} %param.7) | copy-start | bytes 983044
  7.2 278.9 %all-gather.3.cloned.1.call-start = ((), (), s32[]{:S(2)}) async-start(), calls=%async_computation.2 | async-start | bytes 14976000 | tf_op jit(solution)/shard_map/all_gather | solution.py:85
  13.7 13.2 %copy-start.2 = (bf16[1,16,16,640]{3,2,1,0:T(8,128)(2,1)S(1)}, bf16[1,16,16,640]{3,2,1,0:T(8,128)(2,1)}, u32[]{:S(2)}) copy-start(bf16[1,16,16,640]{3,2,1,0:T(8,128)(2,1)} %param.6) | copy-start | bytes 983044
  13.7 14.2 %copy-start.4 = (f32[1,640]{1,0:T(1,128)S(1)}, f32[1,640]{1,0:T(1,128)}, u32[]{:S(2)}) copy-start(f32[1,640]{1,0:T(1,128)} %param.9) | copy-start | bytes 7684
  13.7 14.3 %copy-start.5 = (f32[1,640]{1,0:T(1,128)S(1)}, f32[1,640]{1,0:T(1,128)}, u32[]{:S(2)}) copy-start(f32[1,640]{1,0:T(1,128)} %param.10) | copy-start | bytes 7684
  13.7 305.3 %all-to-all-start = ((bf16[64,90,640]{2,1,0:T(8,128)(2,1)}), bf16[64,90,640]{2,1,0:T(8,128)(2,1)}, u32[]{:S(2)}, u32[]{:S(2)}) async-start(bf16[64,90,640]{2,1,0:T(8,128)(2,1)} %stack.8), calls=%async_computation | async-start | bytes 15728640 | tf_op jit(solution)/shard_map/all_to_all | solution.py:79
  319.1 10.0 %copy-start.6 = (s32[64]{0:T(128)S(1)}, s32[64]{0:T(128)}, u32[]{:S(2)}) copy-start(s32[64]{0:T(128)} %param.11) | copy-start | bytes 772
  319.1 404.2 %all-to-all-start.1 = ((bf16[64,90,640]{2,1,0:T(8,128)(2,1)}), bf16[64,90,640]{2,1,0:T(8,128)(2,1)}, u32[]{:S(2)}, u32[]{:S(2)}) async-start(bf16[64,90,640]{2,1,0:T(8,128)(2,1)} %convert_element_type.71), calls=%async_computation.1 | async-start | bytes 15728640 | tf_op jit(solution)/shard_map/all_to_all | solution.py:102
  702.3 29.4 %collective-permute-start.2 = (bf16[2,640]{1,0:T(2,128)(2,1)S(1)}, bf16[2,640]{1,0:T(2,128)(2,1)S(1)}, u32[]{:S(2)}, u32[]{:S(2)}) collective-permute-start(bf16[2,640]{1,0:T(2,128)(2,1)S(1)} %convert_element_type.76), channel_id=1, source_target_pairs={{0,128},{64,192},{128,0},{192,64},{1,129},{65,193},{129,1},{193,65... | collective-permute-start | bytes 7688 | tf_op jit(solution)/shard_map/ppermute | solution.py:12
  702.4 29.3 %collective-permute-start.3 = (bf16[2,640]{1,0:T(2,128)(2,1)S(1)}, bf16[2,640]{1,0:T(2,128)(2,1)S(1)}, u32[]{:S(2)}, u32[]{:S(2)}) collective-permute-start(bf16[2,640]{1,0:T(2,128)(2,1)S(1)} %convert_element_type.76), channel_id=1, source_target_pairs={{0,64},{64,0},{128,192},{192,128},{1,65},{65,1},{129,193},{193,129... | collective-permute-start | bytes 7688 | tf_op jit(solution)/shard_map/ppermute | solution.py:12
  704.4 11.3 %copy-start.3 = (bf16[1,16,16,640]{3,2,1,0:T(8,128)(2,1)S(1)}, bf16[1,16,16,640]{3,2,1,0:T(8,128)(2,1)}, u32[]{:S(2)}) copy-start(bf16[1,16,16,640]{3,2,1,0:T(8,128)(2,1)} %get-tuple-element.21) | copy-start | bytes 983044
  716.9 19.4 %copy-start.1 = (bf16[1,16,16,640]{3,2,1,0:T(8,128)(2,1)S(1)}, bf16[1,16,16,640]{3,2,1,0:T(8,128)(2,1)}, u32[]{:S(2)}) copy-start(bf16[1,16,16,640]{3,2,1,0:T(8,128)(2,1)} %param.7) | copy-start | bytes 983044
  727.8 7.3 collective-permute-start
  729.6 5.7 collective-permute-start.1
Sparse Core Ops, SparseCore 0:
  12.1 273.8 all-gather.2
